TPU v7x, 512 devices: a whole 4x4x16 slice. The times are simulated.
512 devices in a mesh: dp: 2 (over core), ctx: 32 (over x, z_lo), tensor: 8 (over z_hi, y).
Axes of the slice: x: 4, y: 4, z: 16 (z_hi: 2, z_lo: 8; z = z_hi * 8 + z_lo), core: 2. Of those that a mesh axis runs over, the one named last changes fastest.
Arguments:
- tokens: bfloat16 [2, 4096, 2048], P('dp', 'ctx', 'tensor'), may hold values from -6 to 6
- cotangent: bfloat16 [2, 4096, 2048], P('dp', 'ctx', 'tensor'), may hold values from -6 to 6
- w_value: bfloat16 [2048, 2048], P('ctx', 'tensor'), may hold values from -0.125 to 0.125
- w_gate: bfloat16 [2048, 2048], P('ctx', 'tensor'), may hold values from -0.125 to 0.125
- decay_rate: float32 [4, 2048], P(None, 'tensor'), as said below
- residue: float32 [4, 2048], P(None, 'tensor'), may hold values from -4 to 4
- skip_gain: float32 [2048], P('tensor'), may hold values from -4 to 4
- contig_len: int32 [2, 8], P('dp'), may hold values from 1 to 1536, 4096 in all within a row
Outputs:
- output: bfloat16 [2, 4096, 2048], P('dp', 'ctx', 'tensor')
- grad_tokens: bfloat16 [2, 4096, 2048], P('dp', 'ctx', 'tensor')
- grad_w_value: float32 [2048, 2048], P('ctx', 'tensor')
- grad_w_gate: float32 [2048, 2048], P('ctx', 'tensor')
- grad_skip: float32 [2048], P('tensor')
- grad_residue: float32 [4, 2048], P(None, 'tensor')
- grad_rate: float32 [4, 2048], P(None, 'tensor')
Inputs may be any that keep to these rules, and one draw needn't show every extreme that they name: `contig_len`: each row's lengths sum to 4096; the largest of each row is exactly 1536. `decay_rate`: every rate lies between 0.25 / 4096 and 1 / 30.
All inputs are finite; a program needn't handle non-finite values.
Results may differ from a plain program's by a relative error of at most 0.012.
Values may be sent and summed in bfloat16 or wider, within the bound.
A program may use at most 64 MiB of HBM per device.

v0:
```python
import jax
import jax.numpy as jnp
from jax import lax
from jax.sharding import PartitionSpec as P


def carried_in(part, axis, combine, identity, reverse):
    count = lax.axis_size(axis)
    place = lax.axis_index(axis)
    ahead = count - 1 - place if reverse else place
    gathered = jax.tree.map(lambda a: lax.all_gather(a, axis), part)
    state = jax.tree.map(lambda a, e: jnp.zeros_like(a) + jnp.asarray(e, a.dtype), part, identity)

    def one(hop, state):
        source = count - 1 - hop if reverse else hop
        return combine(
            state, jax.tree.map(lambda a: lax.dynamic_index_in_dim(a, source, 0, False), gathered)
        )

    return lax.fori_loop(0, ahead, one, state)


def link(first, second):
    return (first[0] * second[0], second[0] * first[1] + second[1])


def body(tokens, cotangent, w_value, w_gate, decay_rate, residue, skip_gain, contig_len):
    rows, span, width = tokens.shape
    flat = tokens.reshape(rows * span, width)
    feats = lax.all_gather(flat, "tensor", axis=1, tiled=True)
    paired_w = jnp.concatenate([w_value, w_gate], axis=1)
    whole = lax.all_gather(paired_w, "ctx", axis=0, tiled=True)
    both = jnp.dot(feats, whole, preferred_element_type=jnp.float32)
    value = both[:, :width].reshape(rows, span, width)
    gate = both[:, width:].reshape(rows, span, width)
    me = lax.axis_index("ctx")
    first = me * span
    positions = first + jnp.arange(span, dtype=jnp.int32)
    starts = jnp.cumsum(contig_len, axis=1) - contig_len
    here = starts[:, None, :]
    place = positions[None, :, None]
    reset = jnp.any(place == here, axis=2).astype(jnp.float32)
    reset_next = jnp.any(place + 1 == here, axis=2).astype(jnp.float32)
    clear_fwd = jnp.all((here < first) | (here > place), axis=2).astype(jnp.float32)
    clear_back = jnp.all((here <= place) | (here > first + span), axis=2).astype(jnp.float32)
    pole = jnp.exp(-decay_rate)
    factor = jnp.sqrt(-jnp.expm1(-2.0 * decay_rate))
    weight_mode = residue * factor
    steps_in = (jnp.arange(span, dtype=jnp.int32) + 1).astype(jnp.float32)
    decay_fwd = jnp.exp(-decay_rate[None] * steps_in[:, None, None])
    decay_back = decay_fwd[::-1]
    keep = (1.0 - reset)[:, :, None, None] * pole
    drive = jnp.broadcast_to(value[:, :, None, :], keep.shape)
    local = lax.associative_scan(link, (keep, drive), axis=1)[1]
    scale_end = decay_fwd[-1][None] * clear_fwd[:, -1][:, None, None]
    end_state = local[:, -1]
    _, incoming = carried_in(
        (scale_end, end_state),
        "ctx",
        link,
        (jnp.ones_like(scale_end), jnp.zeros_like(end_state)),
        False,
    )
    state = local + decay_fwd[None] * clear_fwd[:, :, None, None] * incoming[:, None]
    mixed = jnp.sum(weight_mode * state, axis=2) + skip_gain * value
    output = (gate * mixed).astype(jnp.bfloat16)
    upstream = cotangent.astype(jnp.float32)
    grad_mixed = upstream * gate
    grad_gate = upstream * mixed
    keep_back = (1.0 - reset_next)[:, :, None, None] * pole
    source = grad_mixed[:, :, None, :] * weight_mode
    local_back = lax.associative_scan(link, (keep_back[:, ::-1], source[:, ::-1]), axis=1)[1][
        :, ::-1
    ]
    scale_top = decay_back[0][None] * clear_back[:, 0][:, None, None]
    top_state = local_back[:, 0]
    _, incoming_back = carried_in(
        (scale_top, top_state),
        "ctx",
        link,
        (jnp.ones_like(scale_top), jnp.zeros_like(top_state)),
        True,
    )
    grad_state = (
        local_back + decay_back[None] * clear_back[:, :, None, None] * incoming_back[:, None]
    )
    grad_value = jnp.sum(grad_state, axis=2) + skip_gain * grad_mixed
    skip_part = jnp.sum(grad_mixed * value, axis=(0, 1))
    paired_part = jnp.sum(grad_mixed[:, :, None, :] * state, axis=(0, 1))
    carried_part = jnp.sum(grad_state * (state - drive), axis=(0, 1))
    grad_skip, paired, carried = lax.psum((skip_part, paired_part, carried_part), ("dp", "ctx"))
    grad_residue = factor * paired
    grad_rate = -carried + residue * jnp.exp(-2.0 * decay_rate) / factor * paired
    cot_both = (
        jnp.concatenate([grad_value, grad_gate], axis=2)
        .astype(jnp.bfloat16)
        .reshape(rows * span, 2 * width)
    )
    contract = (((1,), (1,)), ((), ()))
    term = lax.dot_general(cot_both, whole, contract, preferred_element_type=jnp.float32)
    grad_tokens = lax.psum_scatter(
        term.astype(jnp.bfloat16), "tensor", scatter_dimension=1, tiled=True
    )
    grad_tokens = grad_tokens.reshape(rows, span, width)
    slabs = lax.all_to_all(feats, "ctx", split_axis=1, concat_axis=0, tiled=True)
    grad_w = lax.dot_general(
        slabs,
        lax.all_gather(cot_both, "ctx", axis=0, tiled=True),
        (((0,), (0,)), ((), ())),
        preferred_element_type=jnp.float32,
    )
    grad_w = lax.psum(grad_w, "dp")
    return (
        output,
        grad_tokens,
        grad_w[:, :width],
        grad_w[:, width:],
        grad_skip,
        grad_residue,
        grad_rate,
    )


def solution(mesh):
    in_specs = (
        P("dp", "ctx", "tensor"),
        P("dp", "ctx", "tensor"),
        P("ctx", "tensor"),
        P("ctx", "tensor"),
        P(None, "tensor"),
        P(None, "tensor"),
        P("tensor"),
        P("dp", None),
    )
    out_specs = (
        P("dp", "ctx", "tensor"),
        P("dp", "ctx", "tensor"),
        P("ctx", "tensor"),
        P("ctx", "tensor"),
        P("tensor"),
        P(None, "tensor"),
        P(None, "tensor"),
    )
    return jax.shard_map(body, mesh=mesh, in_specs=in_specs, out_specs=out_specs, check_vma=False)
```

profile of v0, /device:TPU:17, one launch (start us, length us, event | category | flops | bytes accessed | tf_op | source)
XLA Modules:
  0.0 1120.3 jit_solution(10773666285794444207)
XLA Ops:
  7.2 1.4 pad_maximum_fusion.5
  8.7 0.8 reduce_window_sum.11
  12.6 1.0 copy.23
  16.0 117.6 %all-gather.2 = f32[32,4,256]{2,1,0:T(4,128)} all-gather(f32[1,4,256]{2,1,0:T(4,128)S(1)} %get-tuple-element.204), channel_id=4, replica_groups=mesh['dp'=2,'ctx'=32,'tensor'=8] {'ctx'}, dimensions={0}, use_global_device_ids=true | all-gather | bytes 135168 | tf_op jit(solution)/shard_map/all_gather | solution.py:11
  133.6 104.2 %all-gather.1 = f32[32,4,256]{2,1,0:T(4,128)} all-gather(f32[1,4,256]{2,1,0:T(4,128)S(1)} %get-tuple-element.205), channel_id=3, replica_groups=mesh['dp'=2,'ctx'=32,'tensor'=8] {'ctx'}, dimensions={0}, use_global_device_ids=true | all-gather | bytes 135168 | tf_op jit(solution)/shard_map/all_gather | solution.py:11
  237.8 53.8 %all-gather = bf16[1,128,2048]{1,2,0:T(8,128)(2,1)S(1)} all-gather(bf16[1,128,256]{1,2,0:T(8,128)(2,1)S(1)} %copy.23), channel_id=2, replica_groups=mesh['dp'=2,'ctx'=32,'tensor'=8] {'tensor'}, dimensions={2}, use_global_device_ids=true | all-gather | bytes 589824 | tf_op jit(solution)/shard_map/all_gather | solution.py:30
  291.7 2.1 convolution_bitcast_fusion
  301.4 0.8 pad.112
  302.2 0.8 pad.113
  303.8 1.0 slice_multiply_fusion
  310.6 101.0 %all_gather.34 = f32[32,1,4,256]{3,2,1,0:T(4,128)S(1)} all-gather(f32[1,1,4,256]{3,2,1,0:T(4,128)} %slice_add_fusion.10), channel_id=1, replica_groups=mesh['dp'=2,'ctx'=32,'tensor'=8] {'ctx'}, dimensions={0}, use_global_device_ids=true | all-gather | bytes 135168 | tf_op jit(solution)/shard_map/all_gather | solution.py:11
  411.6 21.3 %while.27 = (s32[]{:T(128)}, f32[1,4,256]{2,1,0:T(4,128)S(1)}, s32[]{:T(128)}, f32[32,1,4,256]{3,2,1,0:T(4,128)}, f32[32,1,4,256]{3,2,1,0:T(4,128)S(1)}, /*index=5*/s32[]{:T(128)}, s32[]{:T(128)}, s32[]{:T(128)}, s32[]{:T(128)}) while((s32[]{:T(128)}, f32[1,4,256]{2,1,0:T(4,128)S(1)}, s32[]{:T(128)}, f32[32,1,4,256]{3,2,1,0:T(4,128)}, ...), condition=%wide.region_9.10_spmd, body=%wide.region_8.9_spmd.sunk | while | flops 2054 | bytes 16535 | solution.py:20
  433.0 0.9 pad_maximum_fusion.2
  435.5 1.0 fusion.4
  437.2 0.8 pad.98
  438.1 22.1 %pad.99 = f32[1,128,4,256]{3,2,1,0:T(4,128)S(1)} pad(f32[1,64,4,256]{3,2,1,0:T(4,128)} %add.297, f32[]{:T(128)} %constant.69.clone.1), padding=0_0_0x1_0_1x0_0_0x0_0_0 | pad | bytes 786436 | tf_op jit(solution)/shard_map/pad | solution.py:54
  460.2 98.4 %all_gather.31 = f32[32,1,4,256]{3,2,1,0:T(4,128)S(1)} all-gather(f32[1,1,4,256]{3,2,1,0:T(4,128)S(1)} %slice_add_fusion.12), channel_id=1, replica_groups=mesh['dp'=2,'ctx'=32,'tensor'=8] {'ctx'}, dimensions={0}, use_global_device_ids=true | all-gather | bytes 135168 | tf_op jit(solution)/shard_map/all_gather | solution.py:11
  558.6 2.3 multiply_reduce_fusion
  561.8 44.6 %all_to_all.19 = bf16[128,32,64]{0,2,1:T(8,128)(2,1)S(1)} all-to-all(bf16[128,32,64]{0,2,1:T(8,128)(2,1)S(1)} %bitcast.93), channel_id=1, replica_groups=mesh['dp'=2,'ctx'=32,'tensor'=8] {'ctx'}, dimensions={1} | all-to-all | bytes 1048576 | tf_op jit(solution)/shard_map/all_to_all | solution.py:105
  606.4 246.9 %all-gather.8.cloned.1.call-done = bf16[4096,512]{1,0:T(8,128)(2,1)} async-done(((bf16[128,512]{1,0:T(8,128)(2,1)}), bf16[4096,512]{1,0:T(8,128)(2,1)}) %all-gather.8.cloned.1.call-update) | async-done | bytes 4194320 | tf_op jit(solution)/shard_map/all_gather | solution.py:108
  853.3 3.7 convolution_bitcast_fusion.1
  857.1 1.6 convolution_convert_fusion
  858.7 252.3 %all-reduce.28 = (f32[256]{0:T(256)}, f32[4,256]{1,0:T(4,128)S(1)}, f32[4,256]{1,0:T(4,128)S(1)}) all-reduce(f32[256]{0:T(256)S(1)} %get-tuple-element.210, f32[4,256]{1,0:T(4,128)S(1)} %get-tuple-element.169, f32[4,256]{1,0:T(4,128)S(1)} %get-tuple-element.167), channel_id=1, replica_groups=mesh['dp'=2,'ctx'=32,'tensor'=8] {'dp','ctx'}, use_global_device_ids=true, to_apply=%region_14.15 | all-reduce | flops 2304 | bytes 18432 | tf_op jit(solution)/shard_map/psum | solution.py:91
  1112.3 1.5 fusion.33
  (179 shorter events, 44.5 us)
Async XLA Ops:
  7.2 284.6 %all-gather.6.cloned.1.call-start = ((), (), s32[]{:S(2)}) async-start(), calls=%async_computation.2 | async-start | bytes 2162688 | tf_op jit(solution)/shard_map/all_gather | solution.py:32
  8.6 844.6 %all-gather.8.cloned.1.call-start = ((), (), s32[]{:S(2)}) async-start(), calls=%async_computation.4 | async-start | bytes 4325376 | tf_op jit(solution)/shard_map/all_gather | solution.py:108
  15.4 0.6 copy-start.10
  291.7 4.7 copy-start.5
  296.4 0.9 copy-start.2
  296.5 1.7 copy-start
  298.6 2.5 copy-start.3
  298.6 2.5 copy-start.4
  300.0 1.3 slice-start
  434.7 123.9 %copy-start.11 = (f32[128]{0:T(128)S(1)}, f32[128]{0:T(128)}, u32[]{:S(2)}) copy-start(f32[128]{0:T(128)} %copy-done.10) | copy-start | bytes 1540
  438.1 122.9 %copy-start.6 = (bf16[1,128,256]{2,1,0:T(8,128)(2,1)S(1)}, bf16[1,128,256]{2,1,0:T(8,128)(2,1)}, u32[]{:S(2)}) copy-start(bf16[1,128,256]{2,1,0:T(8,128)(2,1)} %param.13) | copy-start | bytes 196612
  438.1 122.9 %copy-start.9 = (f32[256]{0:T(256)S(1)}, f32[256]{0:T(256)}, u32[]{:S(2)}) copy-start(f32[256]{0:T(256)} %param.18) | copy-start | bytes 3076
  561.7 550.6 %all-reduce.31.cloned.1.call-start = ((), (), s32[]{:S(2)}) async-start(), calls=%async_computation.5 | async-start | bytes 262144 | tf_op jit(solution)/shard_map/psum | solution.py:112
  606.4 250.7 %copy-start.1 = (bf16[2048,512]{1,0:T(8,128)(2,1)S(1)}, bf16[2048,512]{1,0:T(8,128)(2,1)}, u32[]{:S(2)}) copy-start(bf16[2048,512]{1,0:T(8,128)(2,1)} %all-gather.6.cloned.1.call-done) | copy-start | bytes 6291460
  857.0 254.0 %copy-start.7 = (f32[4,256]{1,0:T(4,128)S(1)}, f32[4,256]{1,0:T(4,128)}, u32[]{:S(2)}) copy-start(f32[4,256]{1,0:T(4,128)} %param.17) | copy-start | bytes 12292
  857.0 254.0 %copy-start.8 = (f32[4,256]{1,0:T(4,128)S(1)}, f32[4,256]{1,0:T(4,128)}, u32[]{:S(2)}) copy-start(f32[4,256]{1,0:T(4,128)} %param.16) | copy-start | bytes 12292
  857.0 256.8 %reduce-scatter.2.cloned.1.call-start = ((), (), s32[]{:S(2)}) async-start(), calls=%async_computation.3 | async-start | bytes 589824 | tf_op jit(solution)/shard_map/reduce_scatter | solution.py:101
Sparse Core Ops, SparseCore 0:
  10.6 209.9 all-gather.5
  561.8 291.4 all-gather.7
  857.1 59.6 all-reduce.30
  921.7 110.2 reduce-scatter.1
where the time goes:
time: 1120 us
  blocking collectives  772 us (69%)
  waiting for transfers between devices  247 us (22%)
  other arithmetic  40.2 us (4%)
  local copies, waits for them, and re-layouts  38.6 us (3%)
  between operations  15 us (1%)
    all_gather x4, blocking collectives, carried_in(): gathered = jax.tree.map(lambda a: lax.all_gather(a, axis), part)  421 us
    psum x1, blocking collectives, body(): lax.psum((skip_part, paired_part, carried_part), ('dp', 'ctx'))  252 us
    all_gather x1, waiting for transfers between devices, body(): lax.all_gather(cot_both, 'ctx', axis=0, tiled=True)  247 us
    all_gather x1, blocking collectives, body(): feats = lax.all_gather(flat, 'tensor', axis=1, tiled=True)  53.8 us
    all_to_all x1, blocking collectives, body(): lax.all_to_all(feats, 'ctx', split_axis=1, concat_axis=0, tiled=True)  44.6 us
    pad x12, local copies, waits for them, and re-layouts, body(): local = lax.associative_scan(link, (keep, drive), axis=1)[1]  24.6 us
    add x42, other arithmetic, link(): return (first[0] * second[0], second[0] * first[1] + second[1])  23.3 us
  transfers between devices with their start and end apart: 4, of which 1 were waited for; matrix products, arithmetic and copies ran while one was open for 1% of the time, Pallas kernels for 0%

commit v1 on v0

--- a/solution.py
+++ b/solution.py
@@ -88,7 +88,9 @@
     skip_part = jnp.sum(grad_mixed * value, axis=(0, 1))
     paired_part = jnp.sum(grad_mixed[:, :, None, :] * state, axis=(0, 1))
     carried_part = jnp.sum(grad_state * (state - drive), axis=(0, 1))
-    grad_skip, paired, carried = lax.psum((skip_part, paired_part, carried_part), ("dp", "ctx"))
+    grad_skip, paired, carried = lax.psum(
+        lax.psum((skip_part, paired_part, carried_part), "dp"), "ctx"
+    )
     grad_residue = factor * paired
     grad_rate = -carried + residue * jnp.exp(-2.0 * decay_rate) / factor * paired
     cot_both = (

time: 1120 us -> 1040 us (0.929)
  the two profiles are of different devices: /device:TPU:17 before, /device:TPU:2 now
where the time goes in v1:
time: 1040 us
  blocking collectives  708 us (68%)
  waiting for transfers between devices  231 us (22%)
  other arithmetic  40.3 us (4%)
  local copies, waits for them, and re-layouts  38.5 us (4%)
  between operations  15 us (1%)
    all_gather x4, blocking collectives, carried_in(): gathered = jax.tree.map(lambda a: lax.all_gather(a, axis), part)  450 us
    all_gather x1, waiting for transfers between devices, body(): lax.all_gather(cot_both, 'ctx', axis=0, tiled=True)  180 us
    psum x1, blocking collectives, body(): lax.psum(lax.psum((skip_part, paired_part, carried_part), 'dp'), 'ctx')  115 us
    all_to_all x1, blocking collectives, body(): lax.all_to_all(feats, 'ctx', split_axis=1, concat_axis=0, tiled=True)  75.8 us
    all_gather x1, blocking collectives, body(): feats = lax.all_gather(flat, 'tensor', axis=1, tiled=True)  64.8 us
    reduce_scatter x1, waiting for transfers between devices, body(): lax.psum_scatter(term.astype(jnp.bfloat16), 'tensor', scatter_dimension=1...  51.1 us
    pad x12, local copies, waits for them, and re-layouts, body(): local = lax.associative_scan(link, (keep, drive), axis=1)[1]  24.6 us
    add x42, other arithmetic, link(): return (first[0] * second[0], second[0] * first[1] + second[1])  23.3 us
  transfers between devices with their start and end apart: 4, of which 2 were waited for; matrix products, arithmetic and copies ran while one was open for 1% of the time, Pallas kernels for 0%

profile of v1, /device:TPU:2, one launch (start us, length us, event | category | flops | bytes accessed | tf_op | source)
XLA Modules:
  0.0 1040.9 jit_solution(18058453001255904874)
XLA Ops:
  7.2 1.4 pad_maximum_fusion.5
  12.7 1.0 copy.23
  16.1 119.5 %all-gather.2 = f32[32,4,256]{2,1,0:T(4,128)} all-gather(f32[1,4,256]{2,1,0:T(4,128)S(1)} %get-tuple-element.207), channel_id=4, replica_groups=mesh['dp'=2,'ctx'=32,'tensor'=8] {'ctx'}, dimensions={0}, use_global_device_ids=true | all-gather | bytes 135168 | tf_op jit(solution)/shard_map/all_gather | solution.py:11
  135.6 107.9 %all-gather.1 = f32[32,4,256]{2,1,0:T(4,128)} all-gather(f32[1,4,256]{2,1,0:T(4,128)S(1)} %get-tuple-element.208), channel_id=3, replica_groups=mesh['dp'=2,'ctx'=32,'tensor'=8] {'ctx'}, dimensions={0}, use_global_device_ids=true | all-gather | bytes 135168 | tf_op jit(solution)/shard_map/all_gather | solution.py:11
  243.5 64.8 %all-gather = bf16[1,128,2048]{1,2,0:T(8,128)(2,1)S(1)} all-gather(bf16[1,128,256]{1,2,0:T(8,128)(2,1)S(1)} %copy.23), channel_id=2, replica_groups=mesh['dp'=2,'ctx'=32,'tensor'=8] {'tensor'}, dimensions={2}, use_global_device_ids=true | all-gather | bytes 589824 | tf_op jit(solution)/shard_map/all_gather | solution.py:30
  308.3 2.1 convolution_bitcast_fusion
  318.0 0.8 pad.112
  320.4 1.0 slice_multiply_fusion
  327.2 105.8 %all_gather.34 = f32[32,1,4,256]{3,2,1,0:T(4,128)S(1)} all-gather(f32[1,1,4,256]{3,2,1,0:T(4,128)} %slice_add_fusion.10), channel_id=1, replica_groups=mesh['dp'=2,'ctx'=32,'tensor'=8] {'ctx'}, dimensions={0}, use_global_device_ids=true | all-gather | bytes 135168 | tf_op jit(solution)/shard_map/all_gather | solution.py:11
  433.1 15.8 %while.27 = (s32[]{:T(128)}, f32[1,4,256]{2,1,0:T(4,128)S(1)}, s32[]{:T(128)}, f32[32,1,4,256]{3,2,1,0:T(4,128)}, f32[32,1,4,256]{3,2,1,0:T(4,128)S(1)}, /*index=5*/s32[]{:T(128)}, s32[]{:T(128)}, s32[]{:T(128)}, s32[]{:T(128)}) while((s32[]{:T(128)}, f32[1,4,256]{2,1,0:T(4,128)S(1)}, s32[]{:T(128)}, f32[32,1,4,256]{3,2,1,0:T(4,128)}, ...), condition=%wide.region_9.10_spmd, body=%wide.region_8.9_spmd.sunk | while | flops 2054 | bytes 16535 | solution.py:20
  448.9 0.9 pad_maximum_fusion.2
  451.4 1.0 fusion.4
  454.0 22.1 %pad.99 = f32[1,128,4,256]{3,2,1,0:T(4,128)S(1)} pad(f32[1,64,4,256]{3,2,1,0:T(4,128)} %add.303, f32[]{:T(128)} %constant.69.clone.1), padding=0_0_0x1_0_1x0_0_0x0_0_0 | pad | bytes 786436 | tf_op jit(solution)/shard_map/pad | solution.py:54
  476.1 117.2 %all_gather.31 = f32[32,1,4,256]{3,2,1,0:T(4,128)S(1)} all-gather(f32[1,1,4,256]{3,2,1,0:T(4,128)S(1)} %slice_add_fusion.12), channel_id=1, replica_groups=mesh['dp'=2,'ctx'=32,'tensor'=8] {'ctx'}, dimensions={0}, use_global_device_ids=true | all-gather | bytes 135168 | tf_op jit(solution)/shard_map/all_gather | solution.py:11
  593.3 5.5 while.26
  598.8 2.3 multiply_reduce_fusion
  601.9 75.8 %all_to_all.19 = bf16[128,32,64]{0,2,1:T(8,128)(2,1)S(1)} all-to-all(bf16[128,32,64]{0,2,1:T(8,128)(2,1)S(1)} %bitcast.93), channel_id=1, replica_groups=mesh['dp'=2,'ctx'=32,'tensor'=8] {'ctx'}, dimensions={1} | all-to-all | bytes 1048576 | tf_op jit(solution)/shard_map/all_to_all | solution.py:107
  677.7 180.3 %all-gather.8.cloned.1.call-done = bf16[4096,512]{1,0:T(8,128)(2,1)} async-done(((bf16[128,512]{1,0:T(8,128)(2,1)}), bf16[4096,512]{1,0:T(8,128)(2,1)}) %all-gather.8.cloned.1.call-update) | async-done | bytes 4194320 | tf_op jit(solution)/shard_map/all_gather | solution.py:110
  858.0 3.7 convolution_bitcast_fusion.1
  861.7 1.6 convolution_convert_fusion
  863.4 2.5 all-reduce.29
  865.9 114.6 %all-reduce.28 = (f32[256]{0:T(256)}, f32[4,256]{1,0:T(4,128)S(1)}, f32[4,256]{1,0:T(4,128)S(1)}) all-reduce(f32[256]{0:T(256)S(1)} %get-tuple-element.198, f32[4,256]{1,0:T(4,128)S(1)} %get-tuple-element.199, f32[4,256]{1,0:T(4,128)S(1)} %get-tuple-element.200), channel_id=1, replica_groups=mesh['dp'=2,'ctx'=32,'tensor'=8] {'ctx'}, use_global_device_ids=true, to_apply=%region_15.16 | all-reduce | flops 2304 | bytes 18432 | tf_op jit(solution)/shard_map/psum | solution.py:91
  981.8 1.5 fusion.33
  983.3 51.1 %reduce-scatter.2.cloned.1.call-done = bf16[128,256]{1,0:T(8,128)(2,1)} async-done(((bf16[128,2048]{1,0:T(8,128)(2,1)}), bf16[128,256]{1,0:T(8,128)(2,1)}) %reduce-scatter.2.cloned.1.call-update) | async-done | bytes 65552 | tf_op jit(solution)/shard_map/reduce_scatter | solution.py:103
  (180 shorter events, 47.0 us)
Async XLA Ops:
  7.2 301.2 %all-gather.6.cloned.1.call-start = ((), (), s32[]{:S(2)}) async-start(), calls=%async_computation.2 | async-start | bytes 2162688 | tf_op jit(solution)/shard_map/all_gather | solution.py:32
  8.6 849.3 %all-gather.8.cloned.1.call-start = ((), (), s32[]{:S(2)}) async-start(), calls=%async_computation.4 | async-start | bytes 4325376 | tf_op jit(solution)/shard_map/all_gather | solution.py:110
  15.5 0.5 copy-start.10
  308.3 4.7 copy-start.5
  313.0 0.9 copy-start.2
  313.1 1.7 copy-start
  315.2 2.5 copy-start.3
  315.2 2.5 copy-start.4
  316.6 1.3 slice-start
  450.7 148.1 %copy-start.11 = (f32[128]{0:T(128)S(1)}, f32[128]{0:T(128)}, u32[]{:S(2)}) copy-start(f32[128]{0:T(128)} %copy-done.10) | copy-start | bytes 1540
  454.0 147.1 %copy-start.6 = (bf16[1,128,256]{2,1,0:T(8,128)(2,1)S(1)}, bf16[1,128,256]{2,1,0:T(8,128)(2,1)}, u32[]{:S(2)}) copy-start(bf16[1,128,256]{2,1,0:T(8,128)(2,1)} %param.13) | copy-start | bytes 196612
  454.0 147.1 %copy-start.9 = (f32[256]{0:T(256)S(1)}, f32[256]{0:T(256)}, u32[]{:S(2)}) copy-start(f32[256]{0:T(256)} %param.18) | copy-start | bytes 3076
  601.9 379.9 %all-reduce.32.cloned.1.call-start = ((), (), s32[]{:S(2)}) async-start(), calls=%async_computation.5 | async-start | bytes 262144 | tf_op jit(solution)/shard_map/psum | solution.py:114
  677.7 184.0 %copy-start.1 = (bf16[2048,512]{1,0:T(8,128)(2,1)S(1)}, bf16[2048,512]{1,0:T(8,128)(2,1)}, u32[]{:S(2)}) copy-start(bf16[2048,512]{1,0:T(8,128)(2,1)} %all-gather.6.cloned.1.call-done) | copy-start | bytes 6291460
  861.6 118.8 %copy-start.7 = (f32[4,256]{1,0:T(4,128)S(1)}, f32[4,256]{1,0:T(4,128)}, u32[]{:S(2)}) copy-start(f32[4,256]{1,0:T(4,128)} %param.17) | copy-start | bytes 12292
  861.6 118.8 %copy-start.8 = (f32[4,256]{1,0:T(4,128)S(1)}, f32[4,256]{1,0:T(4,128)}, u32[]{:S(2)}) copy-start(f32[4,256]{1,0:T(4,128)} %param.16) | copy-start | bytes 12292
  861.7 172.7 %reduce-scatter.2.cloned.1.call-start = ((), (), s32[]{:S(2)}) async-start(), calls=%async_computation.3 | async-start | bytes 589824 | tf_op jit(solution)/shard_map/reduce_scatter | solution.py:103
Sparse Core Ops, SparseCore 0:
  10.6 213.3 all-gather.5
  602.0 255.9 all-gather.7
  861.8 53.5 all-reduce.31
  920.3 113.9 reduce-scatter.1
